TPU v7x, 32 devices: a whole 2x2x4 slice. The times are simulated.
32 devices in a mesh: fsdp: 8 (over z, x), ctx: 4 (over y, core).
Axes of the slice: x: 2, y: 2, z: 4, core: 2. Of those that a mesh axis runs over, the one named last changes fastest.
Arguments:
- tokens: bfloat16 [8, 512, 576], P('fsdp', 'ctx'), may hold values from -6 to 6
- positions: int32 [8, 512], P('fsdp'), may hold values from 0 to 511, as said below
- w_query: bfloat16 [576, 576], P('fsdp'), may hold values from -0.25 to 0.25
- w_key: bfloat16 [576, 192], P('fsdp'), may hold values from -0.25 to 0.25
- w_value: bfloat16 [576, 192], P('fsdp'), may hold values from -0.25 to 0.25
- w_output: bfloat16 [576, 576], P('fsdp'), may hold values from -2 to 2
- w_gate: bfloat16 [576, 1536], P('fsdp'), may hold values from -0.25 to 0.25
- w_up: bfloat16 [576, 1536], P('fsdp'), may hold values from -0.25 to 0.25
- w_down: bfloat16 [1536, 576], P('fsdp'), may hold values from -0.15625 to 0.15625
- gain_attention: bfloat16 [576], P('fsdp'), may hold values from 0.5 to 1.5
- gain_mlp: bfloat16 [576], P('fsdp'), may hold values from 0.5 to 1.5
- cotangent: bfloat16 [8, 512, 576], P('fsdp', 'ctx'), may hold values from -6 to 6
Outputs:
- block_out: bfloat16 [8, 512, 576], P('fsdp', 'ctx')
- grad_tokens: bfloat16 [8, 512, 576], P('fsdp', 'ctx')
- grad_w_query: float32 [576, 576], P('fsdp')
- grad_w_key: float32 [576, 192], P('fsdp')
- value_weight_gradient: float32 [576, 192], P('fsdp')
- grad_w_output: float32 [576, 576], P('fsdp')
- grad_w_gate: float32 [576, 1536], P('fsdp')
- grad_w_up: float32 [576, 1536], P('fsdp')
- grad_w_down: float32 [1536, 576], P('fsdp')
- grad_gain_attention: float32 [576], P('fsdp')
- grad_gain_mlp: float32 [576], P('fsdp')
Inputs may be any that keep to these rules, and one draw needn't show every extreme that they name: In each sequence the positions are a permutation of 0 to 511 made of aligned runs of 64 consecutive positions; the 128 rows that ctx gives one device are two such runs whose run numbers add to 7.
All inputs are finite; a program needn't handle non-finite values.
Results may differ from a plain program's by a relative error of at most 0.02.
Values may be sent and summed in bfloat16 or wider, within the bound.
No kernel may reach another device: no remote copies, remote signals or barrier semaphores. Data moves between devices by JAX's collectives and lax.ppermute only.
A program may use at most 128 MiB of HBM per device.

v0:
```python
import math
import jax
import jax.numpy as jnp
from jax import lax
from jax.sharding import PartitionSpec as P

HEADS = 9
KV_HEADS = 3
HEAD_DIM = 64
NORM_EPS = 1e-05
ROPE_BASE = 100000.0


def matmul(left, right):
    return jnp.dot(left, right, preferred_element_type=jnp.float32)


def rope_tables(position_rows):
    half_size = HEAD_DIM // 2
    frequency = ROPE_BASE ** (-jnp.arange(half_size, dtype=jnp.float32) / half_size)
    angles = position_rows.astype(jnp.float32)[:, None] * frequency[None, :]
    return (jnp.cos(angles)[:, None, :], jnp.sin(angles)[:, None, :])


def rotate(inputs, cos_table, sin_table, inverse):
    row_count = inputs.shape[0]
    halves = inputs.reshape(row_count, -1, 2, HEAD_DIM // 2)
    first_half = halves[:, :, 0]
    second_half = halves[:, :, 1]
    if inverse:
        new_first = first_half * cos_table + second_half * sin_table
        new_second = second_half * cos_table - first_half * sin_table
    else:
        new_first = first_half * cos_table - second_half * sin_table
        new_second = second_half * cos_table + first_half * sin_table
    return jnp.stack([new_first, new_second], axis=2).reshape(row_count, -1)


def norm_forward(inputs, gain):
    scale_row = lax.rsqrt(jnp.mean(inputs * inputs, axis=-1, keepdims=True) + NORM_EPS)
    return (scale_row, inputs * scale_row * gain.astype(jnp.float32))


def norm_backward(inputs, scale_row, gain, grad_normed):
    scaled_grad = grad_normed * gain.astype(jnp.float32)
    grad_gain = jnp.sum(grad_normed * inputs * scale_row, axis=0)
    inner_mean = jnp.mean(scaled_grad * inputs, axis=-1, keepdims=True)
    grad_inputs = scale_row * (scaled_grad - inputs * scale_row * scale_row * inner_mean)
    return (grad_inputs, grad_gain)


def slice_keys(kv_whole, seq_positions, first_row, key_rows):
    kv_width = KV_HEADS * HEAD_DIM
    kv_block = lax.dynamic_slice_in_dim(kv_whole, first_row, key_rows, 0)
    key_pos = lax.dynamic_slice_in_dim(seq_positions, first_row, key_rows, 0)
    key_block = kv_block[:, :kv_width].reshape(key_rows, KV_HEADS, HEAD_DIM)
    value_block = kv_block[:, kv_width:].reshape(key_rows, KV_HEADS, HEAD_DIM)
    return (key_block, value_block, key_pos)


def block_scores(query_heads, key_block, own_pos, key_pos):
    scores = jnp.einsum(
        "tgrd,kgd->grtk", query_heads, key_block, preferred_element_type=jnp.float32
    )
    visible = key_pos[None, :] <= own_pos[:, None]
    return (scores * HEAD_DIM ** (-0.5), visible)


def shards(
    tokens,
    positions,
    w_query,
    w_key,
    w_value,
    w_output,
    w_gate,
    w_up,
    w_down,
    gain_attention,
    gain_mlp,
    cotangent,
):
    single_precision = jnp.float32
    low = jnp.bfloat16
    row_count = tokens.shape[1]
    model_width = tokens.shape[2]
    group_size = HEADS // KV_HEADS
    kv_width = KV_HEADS * HEAD_DIM
    score_scale = HEAD_DIM ** (-0.5)
    x_float = tokens.reshape(row_count, model_width).astype(single_precision)
    cot_rows = cotangent.reshape(row_count, model_width)
    seq_positions = positions.reshape(-1)
    length = seq_positions.shape[0]
    own_pos = lax.dynamic_slice_in_dim(
        seq_positions, lax.axis_index("ctx") * row_count, row_count, 0
    )
    key_rows = math.gcd(length, 256)
    key_steps = length // key_rows
    gathered = (
        lax.all_gather(w_query, "fsdp", axis=0, tiled=True),
        lax.all_gather(w_key, "fsdp", axis=0, tiled=True),
        lax.all_gather(w_value, "fsdp", axis=0, tiled=True),
        lax.all_gather(w_output, "fsdp", axis=0, tiled=True),
        lax.all_gather(w_gate, "fsdp", axis=0, tiled=True),
        lax.all_gather(w_up, "fsdp", axis=0, tiled=True),
        lax.all_gather(w_down, "fsdp", axis=0, tiled=True),
        lax.all_gather(gain_attention, "fsdp", axis=0, tiled=True),
        lax.all_gather(gain_mlp, "fsdp", axis=0, tiled=True),
    )
    (
        query_full,
        key_full,
        value_full,
        output_full,
        gate_full,
        up_full,
        down_full,
        gain_first,
        gain_second,
    ) = gathered
    rms_first, normed = norm_forward(x_float, gain_first)
    normed_first = normed.astype(low)
    cos_table, sin_table = rope_tables(own_pos)
    queries = rotate(matmul(normed_first, query_full), cos_table, sin_table, False).astype(low)
    keys = rotate(matmul(normed_first, key_full), cos_table, sin_table, False).astype(low)
    values = matmul(normed_first, value_full).astype(low)
    local_kv = jnp.concatenate([keys, values], axis=1)
    kv_whole = lax.all_gather(local_kv, "ctx", axis=0, tiled=True)
    query_heads = queries.reshape(row_count, KV_HEADS, group_size, HEAD_DIM)

    def add_totals(index, totals):
        key_block, value_block, key_pos = slice_keys(
            kv_whole, seq_positions, index * key_rows, key_rows
        )
        scores, visible = block_scores(query_heads, key_block, own_pos, key_pos)
        return totals + jnp.sum(jnp.where(visible, jnp.exp(scores), 0.0), axis=-1)

    totals = lax.fori_loop(
        0, key_steps, add_totals, jnp.zeros((KV_HEADS, group_size, row_count), single_precision)
    )
    logsum = jnp.log(totals)

    def add_output(index, running):
        key_block, value_block, key_pos = slice_keys(
            kv_whole, seq_positions, index * key_rows, key_rows
        )
        scores, visible = block_scores(query_heads, key_block, own_pos, key_pos)
        probs = jnp.where(visible, jnp.exp(scores - logsum[..., None]), 0.0).astype(low)
        return running + jnp.einsum(
            "grtk,kgd->tgrd", probs, value_block, preferred_element_type=single_precision
        )

    mixed = lax.fori_loop(
        0,
        key_steps,
        add_output,
        jnp.zeros((row_count, KV_HEADS, group_size, HEAD_DIM), single_precision),
    )
    attended = mixed.reshape(row_count, model_width).astype(low)
    residual = x_float + matmul(attended, output_full)
    rms_second, normed = norm_forward(residual, gain_second)
    normed_second = normed.astype(low)
    gate_values = matmul(normed_second, gate_full)
    up_values = matmul(normed_second, up_full)
    sigmoid_gate = jax.nn.sigmoid(gate_values)
    middle = (gate_values * sigmoid_gate * up_values).astype(low)
    block_out = (residual + matmul(middle, down_full)).astype(low)
    regathered = (
        lax.all_gather(w_query, "fsdp", axis=0, tiled=True),
        lax.all_gather(w_key, "fsdp", axis=0, tiled=True),
        lax.all_gather(w_value, "fsdp", axis=0, tiled=True),
        lax.all_gather(w_output, "fsdp", axis=0, tiled=True),
        lax.all_gather(w_gate, "fsdp", axis=0, tiled=True),
        lax.all_gather(w_up, "fsdp", axis=0, tiled=True),
        lax.all_gather(w_down, "fsdp", axis=0, tiled=True),
        lax.all_gather(gain_attention, "fsdp", axis=0, tiled=True),
        lax.all_gather(gain_mlp, "fsdp", axis=0, tiled=True),
    )
    (
        query_back_w,
        key_back_w,
        value_back_w,
        output_back_w,
        gate_back_w,
        up_back_w,
        down_back_w,
        gain_first_b,
        gain_second_b,
    ) = regathered
    kv_back = lax.all_gather(local_kv, "ctx", axis=0, tiled=True)
    grad_down = matmul(middle.T, cot_rows)
    grad_middle = matmul(cot_rows, down_back_w.T)
    grad_gate = (
        grad_middle * up_values * sigmoid_gate * (1.0 + gate_values * (1.0 - sigmoid_gate))
    ).astype(low)
    grad_up_low = (grad_middle * gate_values * sigmoid_gate).astype(low)
    grad_gate_w = matmul(normed_second.T, grad_gate)
    grad_up_w = matmul(normed_second.T, grad_up_low)
    grad_normed_second = matmul(grad_gate, gate_back_w.T) + matmul(grad_up_low, up_back_w.T)
    grad_resid_norm, grad_gain_mlp = norm_backward(
        residual, rms_second, gain_second_b, grad_normed_second
    )
    grad_residual = cot_rows.astype(single_precision) + grad_resid_norm
    grad_residual_low = grad_residual.astype(low)
    grad_output_w = matmul(attended.T, grad_residual_low)
    grad_attended = matmul(grad_residual_low, output_back_w.T).astype(low)
    attention_head_gradient = grad_attended.reshape(row_count, KV_HEADS, group_size, HEAD_DIM)
    attention_head_rows = attended.reshape(row_count, KV_HEADS, group_size, HEAD_DIM)
    row_correction = jnp.einsum(
        "kzwn->zwk",
        attention_head_gradient.astype(single_precision)
        * attention_head_rows.astype(single_precision),
    )

    def score_grads(key_block, value_block, key_pos):
        scores, visible = block_scores(query_heads, key_block, own_pos, key_pos)
        soft = jnp.where(visible, jnp.exp(scores - logsum[..., None]), 0.0)
        grad_soft = jnp.einsum(
            "tgrd,kgd->grtk",
            attention_head_gradient,
            value_block,
            preferred_element_type=single_precision,
        )
        grad_scores = (soft * (grad_soft - row_correction[..., None]) * score_scale).astype(low)
        return (soft, grad_scores)

    def add_query_grad(index, running):
        key_block, value_block, key_pos = slice_keys(
            kv_back, seq_positions, index * key_rows, key_rows
        )
        soft, grad_scores = score_grads(key_block, value_block, key_pos)
        return running + jnp.einsum(
            "grtk,kgd->tgrd", grad_scores, key_block, preferred_element_type=single_precision
        )

    grad_query_heads = lax.fori_loop(
        0,
        key_steps,
        add_query_grad,
        jnp.zeros((row_count, KV_HEADS, group_size, HEAD_DIM), single_precision),
    )
    sub_rows = math.gcd(row_count * lax.axis_size("ctx"), key_rows)

    def one_piece(piece_index):
        key_block, value_block, key_pos = slice_keys(
            kv_back, seq_positions, piece_index * sub_rows, sub_rows
        )
        soft, grad_scores = score_grads(key_block, value_block, key_pos)
        key_grad = jnp.einsum(
            "grtk,tgrd->kgd", grad_scores, query_heads, preferred_element_type=single_precision
        )
        value_grad = jnp.einsum(
            "grtk,tgrd->kgd",
            soft.astype(low),
            attention_head_gradient,
            preferred_element_type=single_precision,
        )
        return jnp.concatenate(
            [key_grad.reshape(sub_rows, kv_width), value_grad.reshape(sub_rows, kv_width)], axis=1
        )

    pieces = lax.map(
        one_piece, jnp.arange(row_count * lax.axis_size("ctx") // sub_rows, dtype=jnp.int32)
    )
    kv_grads = lax.psum_scatter(
        pieces.reshape(row_count * lax.axis_size("ctx"), 2 * kv_width).astype(jnp.bfloat16),
        "ctx",
        scatter_dimension=0,
        tiled=True,
    ).astype(jnp.float32)
    query_back = rotate(
        grad_query_heads.reshape(row_count, model_width), cos_table, sin_table, True
    ).astype(low)
    key_back = rotate(kv_grads[:, :kv_width], cos_table, sin_table, True).astype(low)
    value_back = kv_grads[:, kv_width:].astype(low)
    grad_query_w = matmul(normed_first.T, query_back)
    grad_key_w = matmul(normed_first.T, key_back)
    grad_value_w = matmul(normed_first.T, value_back)
    grad_normed_first = (
        matmul(query_back, query_back_w.T)
        + matmul(key_back, key_back_w.T)
        + matmul(value_back, value_back_w.T)
    )
    grad_tok_norm, grad_gain_attention = norm_backward(
        x_float, rms_first, gain_first_b, grad_normed_first
    )
    grad_tokens = (grad_residual + grad_tok_norm).astype(low)
    owned = (
        lax.psum_scatter(
            grad_query_w.astype(jnp.bfloat16), "fsdp", scatter_dimension=0, tiled=True
        ).astype(jnp.float32),
        lax.psum_scatter(
            grad_key_w.astype(jnp.bfloat16), "fsdp", scatter_dimension=0, tiled=True
        ).astype(jnp.float32),
        lax.psum_scatter(
            grad_value_w.astype(jnp.bfloat16), "fsdp", scatter_dimension=0, tiled=True
        ).astype(jnp.float32),
        lax.psum_scatter(
            grad_output_w.astype(jnp.bfloat16), "fsdp", scatter_dimension=0, tiled=True
        ).astype(jnp.float32),
        lax.psum_scatter(
            grad_gate_w.astype(jnp.bfloat16), "fsdp", scatter_dimension=0, tiled=True
        ).astype(jnp.float32),
        lax.psum_scatter(
            grad_up_w.astype(jnp.bfloat16), "fsdp", scatter_dimension=0, tiled=True
        ).astype(jnp.float32),
        lax.psum_scatter(
            grad_down.astype(jnp.bfloat16), "fsdp", scatter_dimension=0, tiled=True
        ).astype(jnp.float32),
        lax.psum_scatter(
            grad_gain_attention.astype(jnp.bfloat16), "fsdp", scatter_dimension=0, tiled=True
        ).astype(jnp.float32),
        lax.psum_scatter(
            grad_gain_mlp.astype(jnp.bfloat16), "fsdp", scatter_dimension=0, tiled=True
        ).astype(jnp.float32),
    )
    summed = (
        lax.psum(owned[0].astype(jnp.bfloat16), "ctx").astype(jnp.float32),
        lax.psum(owned[1].astype(jnp.bfloat16), "ctx").astype(jnp.float32),
        lax.psum(owned[2].astype(jnp.bfloat16), "ctx").astype(jnp.float32),
        lax.psum(owned[3].astype(jnp.bfloat16), "ctx").astype(jnp.float32),
        lax.psum(owned[4].astype(jnp.bfloat16), "ctx").astype(jnp.float32),
        lax.psum(owned[5].astype(jnp.bfloat16), "ctx").astype(jnp.float32),
        lax.psum(owned[6].astype(jnp.bfloat16), "ctx").astype(jnp.float32),
        lax.psum(owned[7].astype(jnp.bfloat16), "ctx").astype(jnp.float32),
        lax.psum(owned[8].astype(jnp.bfloat16), "ctx").astype(jnp.float32),
    )
    return (
        block_out.reshape(1, row_count, model_width),
        grad_tokens.reshape(1, row_count, model_width),
        summed[0],
        summed[1],
        summed[2],
        summed[3],
        summed[4],
        summed[5],
        summed[6],
        summed[7],
        summed[8],
    )


def solution(mesh):
    return jax.shard_map(
        shards,
        mesh=mesh,
        in_specs=(
            P("fsdp", "ctx", None),
            P("fsdp", None),
            P("fsdp", None),
            P("fsdp", None),
            P("fsdp", None),
            P("fsdp", None),
            P("fsdp", None),
            P("fsdp", None),
            P("fsdp", None),
            P("fsdp"),
            P("fsdp"),
            P("fsdp", "ctx", None),
        ),
        out_specs=(
            P("fsdp", "ctx", None),
            P("fsdp", "ctx", None),
            P("fsdp", None),
            P("fsdp", None),
            P("fsdp", None),
            P("fsdp", None),
            P("fsdp", None),
            P("fsdp", None),
            P("fsdp", None),
            P("fsdp"),
            P("fsdp"),
        ),
        check_vma=False,
    )
```

profile of v0, /device:TPU:0, one launch (start us, length us, event | category | flops | bytes accessed | tf_op | source)
XLA Modules:
  0.0 731.1 jit_solution(7201682807564454991)
XLA Ops:
  9.5 1.3 fusion.89
  11.5 0.8 dynamic-update-slice
  12.4 0.8 dynamic-update-slice.1
  13.2 23.4 %all-reduce.7 = (bf16[576]{0:T(1024)(128)(2,1)S(1)}, bf16[576]{0:T(1024)(128)(2,1)S(1)}) all-reduce(bf16[576]{0:T(1024)(128)(2,1)S(1)} %dynamic-update-slice, bf16[576]{0:T(1024)(128)(2,1)S(1)} %dynamic-update-slice.1), channel_id=1, replica_groups=mesh['fsdp'=8,'ctx'=4] {'fsdp'}, use_global_device_ids=true, to_apply=%add | all-reduce | flops 1152 | bytes 4608
  36.6 1.0 fusion.60
  37.6 31.9 %all_gather.41 = bf16[576,192]{1,0:T(8,128)(2,1)S(1)} all-gather(bf16[72,192]{1,0:T(8,128)(2,1)} %param.23), channel_id=1, replica_groups=mesh['fsdp'=8,'ctx'=4] {'fsdp'}, dimensions={0}, use_global_device_ids=true | all-gather | bytes 248832 | tf_op jit(solution)/shard_map/all_gather | solution.py:101
  69.7 31.9 %all_gather.42 = bf16[576,192]{1,0:T(8,128)(2,1)S(1)} all-gather(bf16[72,192]{1,0:T(8,128)(2,1)S(1)} %copy-done.44), channel_id=1, replica_groups=mesh['fsdp'=8,'ctx'=4] {'fsdp'}, dimensions={0}, use_global_device_ids=true | all-gather | bytes 248832 | tf_op jit(solution)/shard_map/all_gather | solution.py:102
  102.6 6.4 all_gather.43
  109.1 32.5 %all_gather.44 = bf16[576,576]{1,0:T(8,128)(2,1)S(1)} all-gather(bf16[72,576]{1,0:T(8,128)(2,1)S(1)} %copy-done.40), channel_id=1, replica_groups=mesh['fsdp'=8,'ctx'=4] {'fsdp'}, dimensions={0}, use_global_device_ids=true | all-gather | bytes 746496 | tf_op jit(solution)/shard_map/all_gather | solution.py:100
  142.6 1.4 while.53
  144.1 1.6 while.54
  145.8 33.6 %all_gather.45 = bf16[576,576]{1,0:T(8,128)(2,1)S(1)} all-gather(bf16[72,576]{1,0:T(8,128)(2,1)S(1)} %copy-done.41), channel_id=1, replica_groups=mesh['fsdp'=8,'ctx'=4] {'fsdp'}, dimensions={0}, use_global_device_ids=true | all-gather | bytes 746496 | tf_op jit(solution)/shard_map/all_gather | solution.py:103
  180.0 2.9 fusion.90
  182.9 2.9 fusion.91
  185.8 3.8 multiply_convert_fusion
  190.4 0.9 copy-done.2
  191.3 1.3 multiply_reduce_fusion
  193.7 8.5 %while.52 = (s32[]{:T(128)}, bf16[2,256,384]{2,1,0:T(8,128)(2,1)}, s32[2]{0:T(128)S(1)}, s32[512]{0:T(512)S(1)}, s32[128]{0:T(128)S(1)}, /*index=5*/bf16[512,384...) while((s32[]{:T(128)}, bf16[2,256,384]{2,1,0:T(8,128)(2,1)}, ...), condition=%wide.region_12.13_spmd, body=%wide.region_11.12_spmd.sunk | while | flops 153780224 | bytes 9319195 | solution.py:262
  197.2 0.7 copy-done.32
  201.4 0.7 copy-done.32
  202.2 2.2 convolution_convert_fusion.3
  204.5 2.4 while.55
  207.7 1.3 convolution_convert_fusion.4
  209.1 1.8 convolution_convert_fusion.2
  211.0 0.9 copy-done.13
  211.9 1.8 convolution_convert_fusion.1
  214.0 0.7 copy-done.16
  214.8 2.0 convolution_convert_fusion
  217.9 1.1 fusion.93
  219.0 1.3 reduce-scatter.25.cloned.1.call-done
  220.3 0.8 slice.94
  221.3 1.0 convolution_convert_fusion.6
  222.5 1.5 fusion.47
  224.0 1.0 convolution_convert_fusion.5
  225.8 21.5 %all-reduce.6 = (bf16[576]{0:T(1024)(128)(2,1)S(1)}, bf16[576]{0:T(1024)(128)(2,1)S(1)}) all-reduce(bf16[576]{0:T(1024)(128)(2,1)S(1)} %get-tuple-element.563, bf16[576]{0:T(1024)(128)(2,1)S(1)} %copy-done.48), channel_id=10, replica_groups=mesh['fsdp'=8,'ctx'=4] {'fsdp'}, use_global_device_ids=true, to_apply=%region_30.31.clone | all-reduce | flops 1152 | bytes 4608
  247.5 37.4 %reduce-scatter.29.cloned.1.call-done = bf16[72,576]{1,0:T(8,128)(2,1)} async-done(((bf16[576,576]{1,0:T(8,128)(2,1)}), bf16[72,576]{1,0:T(8,128)(2,1)}) %reduce-scatter.29.cloned.1.call-update) | async-done | bytes 82960
  284.9 63.5 %reduce-scatter.27.cloned.1.call-done = bf16[72,576]{1,0:T(8,128)(2,1)} async-done(((bf16[576,576]{1,0:T(8,128)(2,1)}), bf16[72,576]{1,0:T(8,128)(2,1)}) %reduce-scatter.27.cloned.1.call-update) | async-done | bytes 82960
  348.4 69.0 %reduce-scatter.19.cloned.1.call-done = bf16[72,1536]{1,0:T(8,128)(2,1)} async-done(((bf16[576,1536]{1,0:T(8,128)(2,1)}), bf16[72,1536]{1,0:T(8,128)(2,1)}) %reduce-scatter.19.cloned.1.call-update) | async-done | bytes 221200 | tf_op jit(solution)/shard_map/reduce_scatter | solution.py:301
  417.4 69.0 %reduce-scatter.21.cloned.1.call-done = bf16[72,1536]{1,0:T(8,128)(2,1)} async-done(((bf16[576,1536]{1,0:T(8,128)(2,1)}), bf16[72,1536]{1,0:T(8,128)(2,1)}) %reduce-scatter.21.cloned.1.call-update) | async-done | bytes 221200 | tf_op jit(solution)/shard_map/reduce_scatter | solution.py:304
  486.5 69.8 %reduce-scatter.23.cloned.1.call-done = bf16[192,576]{1,0:T(8,128)(2,1)} async-done(((bf16[1536,576]{1,0:T(8,128)(2,1)}), bf16[192,576]{1,0:T(8,128)(2,1)}) %reduce-scatter.23.cloned.1.call-update) | async-done | bytes 221200 | tf_op jit(solution)/shard_map/reduce_scatter | solution.py:307
  556.2 0.8 fusion.66
  557.1 61.4 %reduce-scatter.15.cloned.1.call-done = bf16[72,192]{1,0:T(8,128)(2,1)} async-done(((bf16[576,192]{1,0:T(8,128)(2,1)}), bf16[72,192]{1,0:T(8,128)(2,1)}) %reduce-scatter.15.cloned.1.call-update) | async-done | bytes 27664 | tf_op jit(solution)/shard_map/reduce_scatter | solution.py:292
  618.4 62.5 %reduce-scatter.17.cloned.1.call-done = bf16[72,192]{1,0:T(8,128)(2,1)} async-done(((bf16[576,192]{1,0:T(8,128)(2,1)}), bf16[72,192]{1,0:T(8,128)(2,1)}) %reduce-scatter.17.cloned.1.call-update) | async-done | bytes 27664 | tf_op jit(solution)/shard_map/reduce_scatter | solution.py:295
  680.9 12.2 %all-reduce.8 = (bf16[72,192]{1,0:T(8,128)(2,1)S(1)}, bf16[72,192]{1,0:T(8,128)(2,1)S(1)}, bf16[72]{0:T(256)(128)(2,1)S(1)}, bf16[72]{0:T(256)(128)(2,1)S(1)}) all-reduce(bf16[72,192]{1,0:T(8,128)(2,1)} %reduce-scatter.15.cloned.1.call-done, ...), channel_id=1, replica_groups=mesh['fsdp'=8,'ctx'=4] {'ctx'}, use_global_device_ids=true, to_apply=%region_18.19 | all-reduce | flops 27792 | bytes 111168 | tf_op jit(solution)/shard_map/psum | solution.py:319
  695.4 23.1 %all-reduce.12.cloned.1.call-done = (bf16[72,576]{1,0:T(8,128)(2,1)}, bf16[72,576]{1,0:T(8,128)(2,1)}, bf16[72,1536]{1,0:T(8,128)(2,1)}, bf16[72,1536]{1,0:T(8,128)(2,1)}, bf16[192,576]{1,0:T(8,128)(2,1)}) async-done(((bf16[72,576]{1,0:T(8,128)(2,1)}, bf16[72,576]{1,0:T(8,128)(2,1)}, bf16[72,1536]{1,0:T(8,128)(2,1)}, bf16[72,1536]{1,0:T(8,128)(2,1)}, bf16[192,576]{1,0:T(8,128)(2,1)}), ...) | async-done | bytes 829456 | tf_op jit(solution)/shard_map/psum | solution.py:318
  718.5 1.8 convert_element_type.260
  720.3 1.7 convert_element_type.256
  722.1 0.8 convert_element_type.258
  (222 shorter events, 24.1 us)
Async XLA Ops:
  7.2 94.4 %copy-start = (bf16[1,128,576]{1,2,0:T(8,128)(2,1)S(1)}, bf16[1,128,576]{1,2,0:T(8,128)(2,1)}, u32[]{:S(2)}) copy-start(bf16[1,128,576]{1,2,0:T(8,128)(2,1)} %param.20) | copy-start | bytes 442372
  7.2 62.5 %copy-start.44 = (bf16[72,192]{1,0:T(8,128)(2,1)S(1)}, bf16[72,192]{1,0:T(8,128)(2,1)}, u32[]{:S(2)}) copy-start(bf16[72,192]{1,0:T(8,128)(2,1)} %param.24) | copy-start | bytes 82948
  7.2 172.8 %all-gather.4.cloned.1.call-start = ((), (), s32[]{:S(2)}) async-start(), calls=%async_computation.8 | async-start | bytes 1990656 | tf_op jit(solution)/shard_map/all_gather | solution.py:104
  7.9 175.0 %all-gather.6.cloned.1.call-start = ((), (), s32[]{:S(2)}) async-start(), calls=%async_computation.9 | async-start | bytes 1990656 | tf_op jit(solution)/shard_map/all_gather | solution.py:105
  8.7 177.1 %all-gather.8.cloned.1.call-start = ((), (), s32[]{:S(2)}) async-start(), calls=%async_computation.10 | async-start | bytes 2211840 | tf_op jit(solution)/shard_map/all_gather | solution.py:106
  9.4 210.9 %reduce-scatter.25.cloned.1.call-start = ((), (), s32[]{:S(2)}) async-start(), calls=%async_computation.16 | async-start | bytes 491520
  36.6 170.5 %copy-start.37 = (f32[576]{0:T(1024)}, f32[576]{0:T(1024)S(1)}, u32[]{:S(2)}) copy-start(f32[576]{0:T(1024)S(1)} %convert_element_type.219) | copy-start | bytes 6916
  36.6 65.8 %copy-start.36 = (s32[1,512]{1,0:T(1,128)S(1)}, s32[1,512]{1,0:T(1,128)}, u32[]{:S(2)}) copy-start(s32[1,512]{1,0:T(1,128)} %param.21) | copy-start | bytes 6148
  37.6 169.5 %copy-start.45 = (f32[128]{0:T(128)}, f32[128]{0:T(128)S(1)}, u32[]{:S(2)}) copy-start(f32[128]{0:T(128)S(1)} %add_rsqrt_fusion.1) | copy-start | bytes 1540
  69.5 33.1 %copy-start.9 = (bf16[576,192]{1,0:T(8,128)(2,1)}, bf16[576,192]{1,0:T(8,128)(2,1)S(1)}, u32[]{:S(2)}) copy-start(bf16[576,192]{1,0:T(8,128)(2,1)S(1)} %all_gather.41) | copy-start | bytes 663556
  69.7 39.3 %copy-start.40 = (bf16[72,576]{1,0:T(8,128)(2,1)S(1)}, bf16[72,576]{1,0:T(8,128)(2,1)}, u32[]{:S(2)}) copy-start(bf16[72,576]{1,0:T(8,128)(2,1)} %param.22) | copy-start | bytes 248836
  102.5 104.4 %copy-start.29 = (f32[128,32]{0,1:T(8,128)}, f32[128,32]{0,1:T(8,128)S(1)}, u32[]{:S(2)}) copy-start(f32[128,32]{0,1:T(8,128)S(1)} %get-tuple-element.662) | copy-start | bytes 49156
  144.0 1.7 copy-start.41
  145.7 34.1 %copy-start.25 = (f32[128,3,3,64]{0,3,2,1:T(8,128)}, f32[128,3,3,64]{0,3,2,1:T(8,128)S(1)}, u32[]{:S(2)}) copy-start(f32[128,3,3,64]{0,3,2,1:T(8,128)S(1)} %get-tuple-element.451) | copy-start | bytes 884740
  145.7 34.1 %copy-start.18 = (bf16[128,3,3,64]{0,3,2,1:T(8,128)(2,1)}, bf16[128,3,3,64]{0,3,2,1:T(8,128)(2,1)S(1)}, u32[]{:S(2)}) copy-start(bf16[128,3,3,64]{0,3,2,1:T(8,128)(2,1)S(1)} %convert_element_type.227) | copy-start | bytes 442372
  180.0 2.9 copy-start.7
  185.8 3.8 copy-start.1
  189.5 1.8 copy-start.2
  191.3 1.3 copy-start.27
  193.6 8.6 %copy-start.19 = (bf16[128,3,3,64]{0,3,2,1:T(8,128)(2,1)S(1)}, bf16[128,3,3,64]{0,3,2,1:T(8,128)(2,1)}, u32[]{:S(2)}) copy-start(bf16[128,3,3,64]{0,3,2,1:T(8,128)(2,1)} %copy-done.18) | copy-start | bytes 442372
  202.1 82.7 %reduce-scatter.29.cloned.1.call-start = ((), (), s32[]{:S(2)}) async-start(), calls=%async_computation.18 | async-start | bytes 829440
  204.5 144.0 %reduce-scatter.27.cloned.1.call-start = ((), (), s32[]{:S(2)}) async-start(), calls=%async_computation.17 | async-start | bytes 829440
  207.0 2.1 copy-start.8
  207.0 2.1 copy-start.15
  209.0 208.4 %reduce-scatter.19.cloned.1.call-start = ((), (), s32[]{:S(2)}) async-start(), calls=%async_computation.13 | async-start | bytes 1990656 | tf_op jit(solution)/shard_map/reduce_scatter | solution.py:301
  211.0 275.5 %reduce-scatter.21.cloned.1.call-start = ((), (), s32[]{:S(2)}) async-start(), calls=%async_computation.14 | async-start | bytes 1990656 | tf_op jit(solution)/shard_map/reduce_scatter | solution.py:304
  213.8 342.4 %reduce-scatter.23.cloned.1.call-start = ((), (), s32[]{:S(2)}) async-start(), calls=%async_computation.15 | async-start | bytes 2211840 | tf_op jit(solution)/shard_map/reduce_scatter | solution.py:307
  216.8 1.1 copy-start.4
  216.8 1.1 copy-start.21
  216.8 4.5 copy-start.30
  216.8 4.5 copy-start.38
  216.8 4.5 copy-start.46
  216.8 401.6 %reduce-scatter.15.cloned.1.call-start = ((), (), s32[]{:S(2)}) async-start(), calls=%async_computation.11 | async-start | bytes 331776 | tf_op jit(solution)/shard_map/reduce_scatter | solution.py:292
  217.9 4.6 copy-start.11
  219.0 3.5 copy-start.17
  222.4 1.6 copy-start.33
  222.4 1.6 copy-start.39
  222.4 1.6 copy-start.47
  222.4 2.7 copy-start.10
  222.4 2.7 copy-start.24
  222.4 458.5 %reduce-scatter.17.cloned.1.call-start = ((), (), s32[]{:S(2)}) async-start(), calls=%async_computation.12 | async-start | bytes 331776 | tf_op jit(solution)/shard_map/reduce_scatter | solution.py:295
  224.0 1.4 copy-start.23
  224.0 1.4 copy-start.34
  225.0 493.5 %all-reduce.12.cloned.1.call-start = ((), (), s32[]{:S(2)}) async-start(), calls=%async_computation.19 | async-start | bytes 1744896 | tf_op jit(solution)/shard_map/psum | solution.py:318
  225.3 330.9 %copy-start.6 = (f32[128,576]{0,1:T(8,128)S(1)}, f32[128,576]{0,1:T(8,128)}, u32[]{:S(2)}) copy-start(f32[128,576]{0,1:T(8,128)} %copy-done.5) | copy-start | bytes 884740
  718.5 3.5 copy-start.35
  718.5 4.3 copy-start.43
  718.5 5.0 copy-start.42
  (15 other events, 13.4 us)
Sparse Core Ops, SparseCore 0:
  10.2 51.9 all-gather.3
  64.3 47.1 all-gather.5
  113.7 56.9 all-gather.7
  202.3 17.9 reduce-scatter.24
  223.5 61.3 reduce-scatter.28
  288.1 60.2 reduce-scatter.26
  351.9 65.4 reduce-scatter.18
  420.9 65.5 reduce-scatter.20
  489.9 66.2 reduce-scatter.22
  559.9 58.4 reduce-scatter.14
  622.3 58.5 reduce-scatter.16
  683.5 34.9 all-reduce.11
where the time goes:
time: 732 us; the launch traced here: 731 us
  waiting for transfers between devices  459 us (63%)
  blocking collectives  193 us (26%)
  matrix products  34.3 us (5%)
  between operations  16.3 us (2%)
  local copies, waits for them, and re-layouts  14 us (2%)
  other arithmetic  11.5 us (2%)
    unnamed x15, waiting for transfers between devices  104 us
    reduce_scatter x1, waiting for transfers between devices, shards(): lax.psum_scatter(grad_down.astype(jnp.bfloat16), 'fsdp', scatter_dimensio...  69.8 us
    reduce_scatter x1, waiting for transfers between devices, shards(): lax.psum_scatter(grad_up_w.astype(jnp.bfloat16), 'fsdp', scatter_dimensio...  69 us
    reduce_scatter x1, waiting for transfers between devices, shards(): lax.psum_scatter(grad_gate_w.astype(jnp.bfloat16), 'fsdp', scatter_dimens...  69 us
    reduce_scatter x1, waiting for transfers between devices, shards(): lax.psum_scatter(grad_value_w.astype(jnp.bfloat16), 'fsdp', scatter_dimen...  62.5 us
    reduce_scatter x1, waiting for transfers between devices, shards(): lax.psum_scatter(grad_key_w.astype(jnp.bfloat16), 'fsdp', scatter_dimensi...  61.4 us
    unnamed x2, blocking collectives  44.8 us
    all_gather x1, blocking collectives, shards(): lax.all_gather(w_output, 'fsdp', axis=0, tiled=True)  33.6 us
  transfers between devices with their start and end apart: 12, of which 9 were waited for; matrix products, arithmetic and copies ran while one was open for 5% of the time, Pallas kernels for 0%

commit v1 on v0

--- a/solution.py
+++ b/solution.py
@@ -315,7 +315,7 @@
         ).astype(jnp.float32),
     )
     summed = (
-        lax.psum(owned[0].astype(jnp.bfloat16), "ctx").astype(jnp.float32),
+        jnp.sum(lax.all_gather(owned[0].astype(jnp.bfloat16), "ctx"), axis=0).astype(jnp.float32),
         lax.psum(owned[1].astype(jnp.bfloat16), "ctx").astype(jnp.float32),
         lax.psum(owned[2].astype(jnp.bfloat16), "ctx").astype(jnp.float32),
         lax.psum(owned[3].astype(jnp.bfloat16), "ctx").astype(jnp.float32),

time: 732 us -> 729 us (level)
    unnamed x15, waiting for transfers between devices: 104 us -> 92.2 us
where the time goes in v1:
time: 729 us; the launch traced here: 728 us
  waiting for transfers between devices  453 us (62%)
  blocking collectives  199 us (27%)
  matrix products  33.2 us (5%)
  between operations  16.1 us (2%)
  local copies, waits for them, and re-layouts  13.3 us (2%)
  other arithmetic  11.5 us (2%)
    unnamed x15, waiting for transfers between devices  92.2 us
    reduce_scatter x1, waiting for transfers between devices, shards(): lax.psum_scatter(grad_down.astype(jnp.bfloat16), 'fsdp', scatter_dimensio...  69.8 us
    reduce_scatter x1, waiting for transfers between devices, shards(): lax.psum_scatter(grad_up_w.astype(jnp.bfloat16), 'fsdp', scatter_dimensio...  69 us
    reduce_scatter x1, waiting for transfers between devices, shards(): lax.psum_scatter(grad_gate_w.astype(jnp.bfloat16), 'fsdp', scatter_dimens...  68.9 us
    reduce_scatter x1, waiting for transfers between devices, shards(): lax.psum_scatter(grad_value_w.astype(jnp.bfloat16), 'fsdp', scatter_dimen...  62.3 us
    reduce_scatter x1, waiting for transfers between devices, shards(): lax.psum_scatter(grad_key_w.astype(jnp.bfloat16), 'fsdp', scatter_dimensi...  61.5 us
    unnamed x2, blocking collectives  42.9 us
    all_gather x1, blocking collectives, shards(): lax.all_gather(w_output, 'fsdp', axis=0, tiled=True)  33.6 us
  transfers between devices with their start and end apart: 12, of which 9 were waited for; matrix products, arithmetic and copies ran while one was open for 5% of the time, Pallas kernels for 0%

profile of v1, /device:TPU:0, one launch (start us, length us, event | category | flops | bytes accessed | tf_op | source)
XLA Modules:
  0.0 728.2 jit_solution(17942261707282635411)
XLA Ops:
  9.5 33.3 %all_gather.48 = bf16[576,192]{1,0:T(8,128)(2,1)S(1)} all-gather(bf16[72,192]{1,0:T(8,128)(2,1)} %param.24), channel_id=1, replica_groups=mesh['fsdp'=8,'ctx'=4] {'fsdp'}, dimensions={0}, use_global_device_ids=true | all-gather | bytes 248832 | tf_op jit(solution)/shard_map/all_gather | solution.py:102
  42.8 1.3 fusion.89
  44.8 0.8 dynamic-update-slice
  45.6 0.8 dynamic-update-slice.1
  46.5 21.5 %all-reduce.7 = (bf16[576]{0:T(1024)(128)(2,1)S(1)}, bf16[576]{0:T(1024)(128)(2,1)S(1)}) all-reduce(bf16[576]{0:T(1024)(128)(2,1)S(1)} %dynamic-update-slice, bf16[576]{0:T(1024)(128)(2,1)S(1)} %dynamic-update-slice.1), channel_id=1, replica_groups=mesh['fsdp'=8,'ctx'=4] {'fsdp'}, use_global_device_ids=true, to_apply=%add | all-reduce | flops 1152 | bytes 4608
  68.1 31.7 %all_gather.47 = bf16[576,192]{1,0:T(8,128)(2,1)S(1)} all-gather(bf16[72,192]{1,0:T(8,128)(2,1)S(1)} %copy-done.34), channel_id=1, replica_groups=mesh['fsdp'=8,'ctx'=4] {'fsdp'}, dimensions={0}, use_global_device_ids=true | all-gather | bytes 248832 | tf_op jit(solution)/shard_map/all_gather | solution.py:101
  101.0 6.5 all_gather.49
  107.5 32.9 %all_gather.50 = bf16[576,576]{1,0:T(8,128)(2,1)S(1)} all-gather(bf16[72,576]{1,0:T(8,128)(2,1)S(1)} %copy-done.32), channel_id=1, replica_groups=mesh['fsdp'=8,'ctx'=4] {'fsdp'}, dimensions={0}, use_global_device_ids=true | all-gather | bytes 746496 | tf_op jit(solution)/shard_map/all_gather | solution.py:100
  141.4 1.4 while.53
  142.9 1.6 while.54
  144.6 33.6 %all_gather.51 = bf16[576,576]{1,0:T(8,128)(2,1)S(1)} all-gather(bf16[72,576]{1,0:T(8,128)(2,1)S(1)} %copy-done.33), channel_id=1, replica_groups=mesh['fsdp'=8,'ctx'=4] {'fsdp'}, dimensions={0}, use_global_device_ids=true | all-gather | bytes 746496 | tf_op jit(solution)/shard_map/all_gather | solution.py:103
  178.9 2.9 fusion.90
  181.8 2.9 fusion.91
  184.7 3.8 multiply_convert_fusion
  189.3 0.9 copy-done.2
  190.2 0.7 multiply_reduce_fusion
  192.0 8.0 %while.52 = (s32[]{:T(128)}, bf16[2,256,384]{2,1,0:T(8,128)(2,1)}, s32[2]{0:T(128)S(1)}, s32[512]{0:T(512)S(1)}, s32[128]{0:T(128)S(1)}, /*index=5*/bf16[512,384...) while((s32[]{:T(128)}, bf16[2,256,384]{2,1,0:T(8,128)(2,1)}, ...), condition=%wide.region_12.13_spmd, body=%wide.region_11.12_spmd.sunk | while | flops 153780224 | bytes 9319203 | solution.py:262
  195.3 0.7 copy-done.27
  199.3 0.7 copy-done.27
  200.1 2.3 convolution_convert_fusion.3
  202.5 1.8 convolution_convert_fusion.2
  204.4 0.9 copy-done.13
  205.3 1.8 convolution_convert_fusion.1
  207.2 0.9 copy-done.16
  208.1 2.0 convolution_convert_fusion
  210.2 8.0 %reduce-scatter.25.cloned.1.call-done = bf16[128,384]{1,0:T(8,128)(2,1)} async-done(((bf16[512,384]{1,0:T(8,128)(2,1)}), bf16[128,384]{1,0:T(8,128)(2,1)}) %reduce-scatter.25.cloned.1.call-update) | async-done | bytes 98320
  218.2 0.8 slice.94
  219.3 1.0 convolution_convert_fusion.6
  220.5 2.4 while.55
  223.0 1.0 convolution_convert_fusion.5
  224.2 1.4 convolution_convert_fusion.4
  226.3 1.5 fusion.47
  229.5 21.3 %all-reduce.6 = (bf16[576]{0:T(1024)(128)(2,1)S(1)}, bf16[576]{0:T(1024)(128)(2,1)S(1)}) all-reduce(bf16[576]{0:T(1024)(128)(2,1)S(1)} %get-tuple-element.563, bf16[576]{0:T(1024)(128)(2,1)S(1)} %get-tuple-element.561), channel_id=11, replica_groups=mesh['fsdp'=8,'ctx'=4] {'fsdp'}, use_global_device_ids=true, to_apply=%region_30.31.clone | all-reduce | flops 1152 | bytes 4608
  250.9 31.9 %reduce-scatter.29.cloned.1.call-done = bf16[72,576]{1,0:T(8,128)(2,1)} async-done(((bf16[576,576]{1,0:T(8,128)(2,1)}), bf16[72,576]{1,0:T(8,128)(2,1)}) %reduce-scatter.29.cloned.1.call-update) | async-done | bytes 82960
  282.8 68.9 %reduce-scatter.19.cloned.1.call-done = bf16[72,1536]{1,0:T(8,128)(2,1)} async-done(((bf16[576,1536]{1,0:T(8,128)(2,1)}), bf16[72,1536]{1,0:T(8,128)(2,1)}) %reduce-scatter.19.cloned.1.call-update) | async-done | bytes 221200 | tf_op jit(solution)/shard_map/reduce_scatter | solution.py:301
  351.7 69.0 %reduce-scatter.21.cloned.1.call-done = bf16[72,1536]{1,0:T(8,128)(2,1)} async-done(((bf16[576,1536]{1,0:T(8,128)(2,1)}), bf16[72,1536]{1,0:T(8,128)(2,1)}) %reduce-scatter.21.cloned.1.call-update) | async-done | bytes 221200 | tf_op jit(solution)/shard_map/reduce_scatter | solution.py:304
  420.7 69.8 %reduce-scatter.23.cloned.1.call-done = bf16[192,576]{1,0:T(8,128)(2,1)} async-done(((bf16[1536,576]{1,0:T(8,128)(2,1)}), bf16[192,576]{1,0:T(8,128)(2,1)}) %reduce-scatter.23.cloned.1.call-update) | async-done | bytes 221200 | tf_op jit(solution)/shard_map/reduce_scatter | solution.py:307
  490.5 0.8 fusion.66
  491.3 61.5 %reduce-scatter.15.cloned.1.call-done = bf16[72,192]{1,0:T(8,128)(2,1)} async-done(((bf16[576,192]{1,0:T(8,128)(2,1)}), bf16[72,192]{1,0:T(8,128)(2,1)}) %reduce-scatter.15.cloned.1.call-update) | async-done | bytes 27664 | tf_op jit(solution)/shard_map/reduce_scatter | solution.py:292
  552.8 62.3 %reduce-scatter.17.cloned.1.call-done = bf16[72,192]{1,0:T(8,128)(2,1)} async-done(((bf16[576,192]{1,0:T(8,128)(2,1)}), bf16[72,192]{1,0:T(8,128)(2,1)}) %reduce-scatter.17.cloned.1.call-update) | async-done | bytes 27664 | tf_op jit(solution)/shard_map/reduce_scatter | solution.py:295
  615.1 11.4 %all-reduce.8 = (bf16[72,192]{1,0:T(8,128)(2,1)S(1)}, bf16[72,192]{1,0:T(8,128)(2,1)S(1)}, bf16[72]{0:T(256)(128)(2,1)S(1)}, bf16[72]{0:T(256)(128)(2,1)S(1)}) all-reduce(bf16[72,192]{1,0:T(8,128)(2,1)} %reduce-scatter.15.cloned.1.call-done, ...), channel_id=1, replica_groups=mesh['fsdp'=8,'ctx'=4] {'ctx'}, use_global_device_ids=true, to_apply=%region_18.19 | all-reduce | flops 27792 | bytes 111168 | tf_op jit(solution)/shard_map/psum | solution.py:319
  628.9 50.1 %reduce-scatter.27.cloned.1.call-done = bf16[72,576]{1,0:T(8,128)(2,1)} async-done(((bf16[576,576]{1,0:T(8,128)(2,1)}), bf16[72,576]{1,0:T(8,128)(2,1)}) %reduce-scatter.27.cloned.1.call-update) | async-done | bytes 82960
  679.0 6.5 all-gather
  686.2 29.3 %all-reduce.12.cloned.1.call-done = (bf16[72,576]{1,0:T(8,128)(2,1)}, bf16[72,1536]{1,0:T(8,128)(2,1)}, bf16[72,1536]{1,0:T(8,128)(2,1)}, bf16[192,576]{1,0:T(8,128)(2,1)}) async-done(((bf16[72,576]{1,0:T(8,128)(2,1)}, bf16[72,1536]{1,0:T(8,128)(2,1)}, bf16[72,1536]{1,0:T(8,128)(2,1)}, bf16[192,576]{1,0:T(8,128)(2,1)}), (bf16[72,576]{1,0:T(8,128)(2,1)}, bf16[72,1536]{1,0:T(8,128)(2,1)}, ...) | async-done | bytes 746512 | tf_op jit(solution)/shard_map/psum | solution.py:321
  715.5 1.6 convert_element_type.256
  717.1 1.7 convert_element_type.258
  718.8 1.7 convert_element_type.260
  720.6 0.8 convert_element_type.262
  (200 shorter events, 23.1 us)
Async XLA Ops:
  7.2 60.8 %copy-start = (bf16[1,128,576]{1,2,0:T(8,128)(2,1)S(1)}, bf16[1,128,576]{1,2,0:T(8,128)(2,1)}, u32[]{:S(2)}) copy-start(bf16[1,128,576]{1,2,0:T(8,128)(2,1)} %param.20) | copy-start | bytes 442372
  7.2 60.9 %copy-start.34 = (bf16[72,192]{1,0:T(8,128)(2,1)S(1)}, bf16[72,192]{1,0:T(8,128)(2,1)}, u32[]{:S(2)}) copy-start(bf16[72,192]{1,0:T(8,128)(2,1)} %param.23) | copy-start | bytes 82948
  7.2 171.7 %all-gather.5.cloned.1.call-start = ((), (), s32[]{:S(2)}) async-start(), calls=%async_computation.8 | async-start | bytes 1990656 | tf_op jit(solution)/shard_map/all_gather | solution.py:104
  7.9 173.9 %all-gather.7.cloned.1.call-start = ((), (), s32[]{:S(2)}) async-start(), calls=%async_computation.9 | async-start | bytes 1990656 | tf_op jit(solution)/shard_map/all_gather | solution.py:105
  8.7 176.0 %all-gather.9.cloned.1.call-start = ((), (), s32[]{:S(2)}) async-start(), calls=%async_computation.10 | async-start | bytes 2211840 | tf_op jit(solution)/shard_map/all_gather | solution.py:106
  9.4 208.8 %reduce-scatter.25.cloned.1.call-start = ((), (), s32[]{:S(2)}) async-start(), calls=%async_computation.16 | async-start | bytes 491520
  9.5 91.3 %copy-start.31 = (s32[1,512]{1,0:T(1,128)S(1)}, s32[1,512]{1,0:T(1,128)}, u32[]{:S(2)}) copy-start(s32[1,512]{1,0:T(1,128)} %param.21) | copy-start | bytes 6148
  42.8 58.2 %copy-start.20 = (bf16[576,192]{1,0:T(8,128)(2,1)}, bf16[576,192]{1,0:T(8,128)(2,1)S(1)}, u32[]{:S(2)}) copy-start(bf16[576,192]{1,0:T(8,128)(2,1)S(1)} %all_gather.48) | copy-start | bytes 663556
  99.8 1.1 copy-start.9
  99.8 7.6 %copy-start.32 = (bf16[72,576]{1,0:T(8,128)(2,1)S(1)}, bf16[72,576]{1,0:T(8,128)(2,1)}, u32[]{:S(2)}) copy-start(bf16[72,576]{1,0:T(8,128)(2,1)} %param.22) | copy-start | bytes 248836
  140.4 0.9 copy-start.3
  142.9 1.7 copy-start.33
  144.5 34.1 %copy-start.22 = (f32[128,3,3,64]{0,3,2,1:T(8,128)}, f32[128,3,3,64]{0,3,2,1:T(8,128)S(1)}, u32[]{:S(2)}) copy-start(f32[128,3,3,64]{0,3,2,1:T(8,128)S(1)} %get-tuple-element.451) | copy-start | bytes 884740
  144.6 34.1 %copy-start.18 = (bf16[128,3,3,64]{0,3,2,1:T(8,128)(2,1)}, bf16[128,3,3,64]{0,3,2,1:T(8,128)(2,1)S(1)}, u32[]{:S(2)}) copy-start(bf16[128,3,3,64]{0,3,2,1:T(8,128)(2,1)S(1)} %convert_element_type.229) | copy-start | bytes 442372
  178.7 3.1 copy-start.35
  178.9 3.0 copy-start.7
  184.7 3.8 copy-start.1
  188.4 0.9 copy-start.12
  188.5 1.8 copy-start.2
  188.5 1.8 copy-start.36
  190.2 0.9 copy-start.24
  191.0 1.0 copy-start.23
  192.0 8.1 %copy-start.19 = (bf16[128,3,3,64]{0,3,2,1:T(8,128)(2,1)S(1)}, bf16[128,3,3,64]{0,3,2,1:T(8,128)(2,1)}, u32[]{:S(2)}) copy-start(bf16[128,3,3,64]{0,3,2,1:T(8,128)(2,1)} %copy-done.18) | copy-start | bytes 442372
  194.2 1.0 copy-start.26
  195.3 0.7 copy-start.27
  198.2 1.0 copy-start.26
  200.0 2.4 copy-start.8
  200.0 2.4 copy-start.15
  200.0 82.8 %reduce-scatter.29.cloned.1.call-start = ((), (), s32[]{:S(2)}) async-start(), calls=%async_computation.18 | async-start | bytes 829440
  202.4 149.3 %reduce-scatter.19.cloned.1.call-start = ((), (), s32[]{:S(2)}) async-start(), calls=%async_computation.13 | async-start | bytes 1990656 | tf_op jit(solution)/shard_map/reduce_scatter | solution.py:301
  204.3 1.0 copy-start.13
  204.3 216.3 %reduce-scatter.21.cloned.1.call-start = ((), (), s32[]{:S(2)}) async-start(), calls=%async_computation.14 | async-start | bytes 1990656 | tf_op jit(solution)/shard_map/reduce_scatter | solution.py:304
  207.1 1.0 copy-start.16
  207.1 1.0 copy-start.25
  207.1 283.4 %reduce-scatter.23.cloned.1.call-start = ((), (), s32[]{:S(2)}) async-start(), calls=%async_computation.15 | async-start | bytes 2211840 | tf_op jit(solution)/shard_map/reduce_scatter | solution.py:307
  210.2 342.7 %reduce-scatter.15.cloned.1.call-start = ((), (), s32[]{:S(2)}) async-start(), calls=%async_computation.11 | async-start | bytes 331776 | tf_op jit(solution)/shard_map/reduce_scatter | solution.py:292
  220.3 394.9 %reduce-scatter.17.cloned.1.call-start = ((), (), s32[]{:S(2)}) async-start(), calls=%async_computation.12 | async-start | bytes 331776 | tf_op jit(solution)/shard_map/reduce_scatter | solution.py:295
  220.5 2.4 copy-start.28
  224.0 454.9 %reduce-scatter.27.cloned.1.call-start = ((), (), s32[]{:S(2)}) async-start(), calls=%async_computation.17 | async-start | bytes 829440
  224.1 2.2 copy-start.11
  224.1 2.2 copy-start.17
  225.6 489.9 %all-reduce.12.cloned.1.call-start = ((), (), s32[]{:S(2)}) async-start(), calls=%async_computation.19 | async-start | bytes 1560576 | tf_op jit(solution)/shard_map/psum | solution.py:321
  226.3 1.5 copy-start.4
  227.7 1.0 copy-start.10
  227.7 1.2 copy-start.21
  227.8 1.2 copy-start.29
  229.0 261.6 %copy-start.6 = (f32[128,576]{0,1:T(8,128)S(1)}, f32[128,576]{0,1:T(8,128)}, u32[]{:S(2)}) copy-start(f32[128,576]{0,1:T(8,128)} %copy-done.5) | copy-start | bytes 884740
  715.5 5.1 copy-start.30
  (3 other events, 2.2 us)
Sparse Core Ops, SparseCore 0:
  10.2 49.4 all-gather.4
  61.9 45.7 all-gather.6
  109.9 57.8 all-gather.8
  200.2 18.0 reduce-scatter.24
  221.5 61.3 reduce-scatter.28
  286.1 65.5 reduce-scatter.18
  355.2 65.4 reduce-scatter.20
  424.1 66.3 reduce-scatter.22
  494.4 58.4 reduce-scatter.14
  556.6 58.5 reduce-scatter.16
  618.5 60.4 reduce-scatter.26
  681.4 34.0 all-reduce.11
